TPU v7x, 32 devices: a whole 2x2x4 slice. The times are simulated.
32 devices in a mesh: groups: 2 (over y), blk: 4 (over z), leaf: 2 (over x), sample: 2 (over core).
Axes of the slice: x: 2, y: 2, z: 4, core: 2. Of those that a mesh axis runs over, the one named last changes fastest.
Arguments:
- residual: float32 [256, 128, 256], P(('groups', 'blk', 'leaf'), 'sample'), parts along dimension 0, may hold values from -60 to 60
- direction: bfloat16 [256, 128, 256], P(('groups', 'blk', 'leaf'), 'sample'), parts along dimension 0, may hold values from -60 to 60
- step: float32 [256], P(('groups', 'sample')), parts along dimension 0, may hold values from 0.2 to 0.8
- coords: bfloat16 [256, 3, 256], P(('groups', 'blk', 'leaf')), parts along dimension 0, may hold values from 0 to 1
- order: int32 [256, 256], P(('groups', 'blk', 'leaf')), parts along dimension 0, may hold values from 0 to 255, each once within a row
- basis: bfloat16 [256, 64, 256], P(('groups', 'blk', 'leaf')), parts along dimension 0, may hold values from -0.5 to 0.5
- leaf_transfer: bfloat16 [256, 64, 64], P(('groups', 'blk', 'leaf')), parts along dimension 0, may hold values from -0.75 to 0.75
- node_transfer: bfloat16 [16, 64, 64], P(('groups', 'blk', 'leaf')), parts along dimension 0, may hold values from -0.75 to 0.75
- near_list: int32 [256, 12], P(('groups', 'blk', 'leaf')), parts along dimension 0, may hold values from 0 to 127, as said below
- coupling_list: int32 [256, 8], P(('groups', 'blk', 'leaf')), parts along dimension 0, may hold values from 0 to 127, as said below
- coupling: bfloat16 [256, 8, 64, 64], P(('groups', 'blk', 'leaf')), parts along dimension 0, may hold values from -0.25 to 0.25
- top_list: int32 [8, 4], P(('groups', 'blk')), parts along dimension 0, may hold values from 0 to 3, as said below
- top_coupling: bfloat16 [8, 4, 64, 64], P(('groups', 'blk')), parts along dimension 0, may hold values from -0.0625 to 0.0625
Outputs:
- residual_next: float32 [256, 128, 256], P(('groups', 'blk', 'leaf'), 'sample'), parts along dimension 0
- direction_next: bfloat16 [256, 128, 256], P(('groups', 'blk', 'leaf'), 'sample'), parts along dimension 0
There are 2 independent parts, one for each index of `groups`. A program takes and returns all parts, laid end to end along the dimension named above; each array names one. Nothing has to cross between parts.
Inputs may be any that keep to these rules, and one draw needn't show every extreme that they name: `near_list`: entry 0 of leaf g is g itself; the other entries are distinct leaves other than g, each at most 16 positions from g around the cycle of 128 leaves; some leaf names both g - 16 and g + 16 (mod 128). `coupling_list`: the entries of leaf g are distinct leaves of the aligned blocks of 16 leaves just before and just after g's own block, around the cycle of 128 leaves, each more than 16 positions from g. `top_list`: the entries of top cluster b name clusters other than b; they may repeat.
All inputs are finite; a program needn't handle non-finite values.
Results may differ from a plain program's by a relative error of at most 0.0065.
Values may be sent and summed in bfloat16 or wider, within the bound.
No kernel may reach another device: no remote copies, remote signals or barrier semaphores. Data moves between devices by JAX's collectives and lax.ppermute only.
A program may use at most 64 MiB of HBM per device.

v0:
```python
import math
import jax
import jax.numpy as jnp
from jax import lax
from jax.sharding import PartitionSpec as P

LEAF_DEV = 16
ROOT_THREE = math.sqrt(3.0)
LENGTH = 0.3
AMPLITUDE = 0.25
NUGGET = 0.5


def padded(array, sides, width):
    for axis, dim in sides:
        count, length = (lax.axis_size(axis), array.shape[dim])
        up = [(i, (i + 1) % count) for i in range(count)]
        down = [(j, i) for i, j in up]
        last = lax.slice_in_dim(array, length - width, length, axis=dim)
        initial = lax.slice_in_dim(array, 0, width, axis=dim)
        before = lax.ppermute(last, axis, up)
        after = lax.ppermute(initial, axis, down)
        array = jnp.concatenate([before, array, after], axis=dim)
    return array


def swapped(array, axis, bit):
    return lax.ppermute(array, axis, [(i, i ^ 1 << bit) for i in range(lax.axis_size(axis))])


def matern(own_offsets, near_offsets, gap_leaves, spread):
    gap_x = (
        own_offsets[0][:, None] - near_offsets[0][None, :] + gap_leaves.astype(jnp.float32) * spread
    )
    gap_y = own_offsets[1][:, None] - near_offsets[1][None, :]
    gap_z = own_offsets[2][:, None] - near_offsets[2][None, :]
    scaled = jnp.sqrt(gap_x * gap_x + gap_y * gap_y + gap_z * gap_z) * (ROOT_THREE / LENGTH)
    return AMPLITUDE * (1.0 + scaled) * jnp.exp(-scaled)


def tile_block(own_offsets, near_offsets, gap_leaves, spread):
    inner = jax.vmap(matern, in_axes=(None, 0, 0, None))
    return jax.vmap(inner, in_axes=(0, 0, 0, None))(own_offsets, near_offsets, gap_leaves, spread)


def on_device(
    residual,
    direction,
    step,
    coords,
    order,
    basis,
    leaf_transfer,
    node_transfer,
    near_list,
    coupling_list,
    coupling,
    top_list,
    top_coupling,
):
    leaf_dev = direction.shape[0]
    samples = direction.shape[1]
    points = direction.shape[2]
    blk_count = lax.axis_size("blk")
    leaf_count = lax.axis_size("leaf")
    leaf_total = leaf_dev * blk_count * leaf_count
    device = lax.axis_index("blk") * leaf_count + lax.axis_index("leaf")
    first_leaf = device * leaf_dev
    spread = 0.5 / LEAF_DEV
    old_norm = lax.psum(jnp.sum(residual * residual, axis=(0, 2)), ("blk", "leaf"))
    packed = jnp.concatenate([direction, coords], axis=1)
    widened = padded(packed, ((("blk", "leaf"), 0),), leaf_dev)
    anchor = first_leaf - leaf_dev
    own_offsets_all = coords.astype(jnp.float32)
    slot_ids = jnp.mod(near_list - anchor, leaf_total)
    window_values = widened[:, :samples, :]
    window_offsets = widened[:, samples:, :]
    half_rows = leaf_dev // 2
    side = lax.axis_index("sample")
    partner_values = swapped(window_values, "sample", 0)
    all_columns = jnp.where(
        side == 0,
        jnp.concatenate([window_values, partner_values], axis=1),
        jnp.concatenate([partner_values, window_values], axis=1),
    )
    base = side * half_rows
    blocks = 4
    columns = all_columns.shape[1]

    def near_block(block_index):
        start_at = base + block_index * blocks
        slot_rows = lax.dynamic_slice_in_dim(slot_ids, start_at, blocks, 0)
        name_rows = lax.dynamic_slice_in_dim(near_list, start_at, blocks, 0)
        leaf_ids = first_leaf + start_at + jnp.arange(blocks, dtype=jnp.int32)
        near_values = all_columns[slot_rows]
        near_offsets = window_offsets[slot_rows].astype(jnp.float32)
        own_offsets = lax.dynamic_slice_in_dim(own_offsets_all, start_at, blocks, 0)
        gap_leaves = (
            jnp.mod(leaf_ids[:, None] - name_rows + leaf_total // 2, leaf_total) - leaf_total // 2
        )
        kernel_tiles = tile_block(own_offsets, near_offsets, gap_leaves, spread).astype(
            jnp.bfloat16
        )
        return jnp.einsum(
            "lkab,lksb->lsa", kernel_tiles, near_values, preferred_element_type=jnp.float32
        )

    mapped = lax.map(near_block, jnp.arange(half_rows // blocks, dtype=jnp.int32))
    own_rows = mapped.reshape(half_rows, columns, points)
    kept_part = lax.dynamic_slice_in_dim(own_rows, side * samples, samples, 1)
    given_part = lax.dynamic_slice_in_dim(own_rows, (1 - side) * samples, samples, 1)
    received = swapped(given_part.astype(jnp.bfloat16), "sample", 0).astype(given_part.dtype)
    near_field = jnp.where(
        side == 0,
        jnp.concatenate([kept_part, received], axis=0),
        jnp.concatenate([received, kept_part], axis=0),
    )
    inverse = jnp.argsort(order, axis=1)
    natural_values = jnp.take_along_axis(basis, inverse[:, None, :], axis=2)
    expansion_weights = jnp.einsum(
        "ejt,ekt->ekj", natural_values, direction, preferred_element_type=jnp.float32
    ).astype(jnp.bfloat16)
    node_coef = jnp.einsum(
        "lrk,lsk->sr", leaf_transfer, expansion_weights, preferred_element_type=jnp.float32
    ).astype(jnp.bfloat16)
    lifted = jnp.einsum(
        "rk,sk->sr", node_transfer[0], node_coef, preferred_element_type=jnp.float32
    )
    top_node = lax.psum(lifted, "leaf").astype(jnp.bfloat16)
    every_top = lax.all_gather(top_node[None], "blk", axis=0, tiled=True)
    chosen = every_top[top_list[0]]
    incoming = jnp.einsum(
        "krj,ksj->sr", top_coupling[0], chosen, preferred_element_type=jnp.float32
    )
    incoming = incoming.astype(jnp.bfloat16)
    down_coef = jnp.einsum(
        "rk,sr->sk", node_transfer[0], incoming, preferred_element_type=jnp.float32
    ).astype(jnp.bfloat16)
    coef_wide = padded(expansion_weights, ((("blk", "leaf"), 0),), leaf_dev)
    paired_block = coef_wide[jnp.mod(coupling_list - (first_leaf - leaf_dev), leaf_total)]
    upward_gathered = jnp.einsum(
        "lrk,sr->lsk", leaf_transfer, down_coef, preferred_element_type=jnp.float32
    )
    upward_gathered = upward_gathered + jnp.einsum(
        "ohvd,ohgd->ogv", coupling, paired_block, preferred_element_type=jnp.float32
    )
    upward_gathered = upward_gathered.astype(jnp.bfloat16)
    distant_field = jnp.einsum(
        "bfw,baf->baw", natural_values, upward_gathered, preferred_element_type=jnp.float32
    )
    product_image = NUGGET * direction.astype(jnp.float32) + near_field + distant_field
    residual_next = residual - step[None, :, None] * product_image
    new_square = jnp.sum(residual_next * residual_next, axis=(0, 2))
    new_norm = lax.psum(new_square, ("blk", "leaf"))
    beta_ratio = new_norm / old_norm
    direction_next = (
        residual_next + beta_ratio[None, :, None] * direction.astype(jnp.float32)
    ).astype(jnp.bfloat16)
    return (residual_next, direction_next)


def solution(mesh):
    in_specs = (
        P(("groups", "blk", "leaf"), "sample", None),
        P(("groups", "blk", "leaf"), "sample", None),
        P(("groups", "sample")),
        P(("groups", "blk", "leaf"), None, None),
        P(("groups", "blk", "leaf"), None),
        P(("groups", "blk", "leaf"), None, None),
        P(("groups", "blk", "leaf"), None, None),
        P(("groups", "blk", "leaf"), None, None),
        P(("groups", "blk", "leaf"), None),
        P(("groups", "blk", "leaf"), None),
        P(("groups", "blk", "leaf"), None, None, None),
        P(("groups", "blk"), None),
        P(("groups", "blk"), None, None, None),
    )
    out_specs = (
        P(("groups", "blk", "leaf"), "sample", None),
        P(("groups", "blk", "leaf"), "sample", None),
    )
    return jax.shard_map(
        on_device, mesh=mesh, in_specs=in_specs, out_specs=out_specs, check_vma=False
    )
```

profile of v0, /device:TPU:0, one launch (start us, length us, event | category | flops | bytes accessed | tf_op | source)
XLA Modules:
  0.0 217.3 jit_solution(16189384715876912534)
XLA Ops:
  10.1 2.9 %collective-permute-start = (bf16[16,67,256]{2,0,1:T(8,128)(2,1)S(1)}, bf16[16,67,256]{2,0,1:T(8,128)(2,1)S(1)}, u32[]{:S(2)}, u32[]{:S(2)}) collective-permute-start(bf16[16,67,256]{2,0,1:T(8,128)(2,1)S(1)} %get-tuple-element.173), channel_id=1, source_target_pairs={{0,2},{2,4},{4,6},{6,8},{8,10},{10,12},{12,14},{14,0},{1,3},{3,5},... | collective-permute-start | bytes 1646600 | tf_op jit(solution)/shard_map/ppermute | solution.py:21
  13.1 3.0 %collective-permute-start.1 = (bf16[16,67,256]{2,0,1:T(8,128)(2,1)S(1)}, bf16[16,67,256]{2,0,1:T(8,128)(2,1)}, u32[]{:S(2)}, u32[]{:S(2)}) collective-permute-start(bf16[16,67,256]{2,0,1:T(8,128)(2,1)S(1)} %get-tuple-element.173), channel_id=1, source_target_pairs={{2,0},{4,2},{6,4},{8,6},{10,8},{12,10},{14,12},{0,14},{3,1},{5,3},... | collective-permute-start | bytes 1646600 | tf_op jit(solution)/shard_map/ppermute | solution.py:22
  17.6 1.9 multiply_reduce_fusion
  20.2 16.4 %collective-permute-done = bf16[16,67,256]{2,0,1:T(8,128)(2,1)S(1)} collective-permute-done((bf16[16,67,256]{2,0,1:T(8,128)(2,1)S(1)}, bf16[16,67,256]{2,0,1:T(8,128)(2,1)S(1)}, u32[]{:S(2)}, u32[]{:S(2)}) %collective-permute-start) | collective-permute-done | bytes 548896 | tf_op jit(solution)/shard_map/ppermute | solution.py:21
  36.5 2.3 %collective-permute-done.1 = bf16[16,67,256]{2,0,1:T(8,128)(2,1)} collective-permute-done((bf16[16,67,256]{2,0,1:T(8,128)(2,1)S(1)}, bf16[16,67,256]{2,0,1:T(8,128)(2,1)}, u32[]{:S(2)}, u32[]{:S(2)}) %collective-permute-start.1) | collective-permute-done | bytes 548896 | tf_op jit(solution)/shard_map/ppermute | solution.py:22
  45.4 40.6 %gather_fusion.4 = bf16[4096,64]{1,0:T(8,128)(2,1)} fusion(bf16[16,64,256]{1,2,0:T(8,128)(2,1)S(1)} %copy.38, s32[4096]{0:T(1024)S(1)} %bitcast.104), kind=kCustom, calls=%fused_computation.4 | custom fusion | bytes 1081344 | tf_op jit(solution)/shard_map/jit(take_along_axis)/gather | solution.py:119
  86.0 2.4 %copy.39 = bf16[16,256,64]{1,2,0:T(8,128)(2,1)} copy(bf16[16,256,64]{2,1,0:T(8,128)(2,1)} %bitcast.109) | data formatting | bytes 1048576 | tf_op jit(solution)/shard_map/jit(take_along_axis)/gather | solution.py:119
  88.4 2.2 %fusion.12 = bf16[16,64,64]{1,2,0:T(8,128)(2,1)} fusion(bf16[16,64,256]{2,1,0:T(8,128)(2,1)} %param.16, bf16[16,256,64]{1,2,0:T(8,128)(2,1)} %copy.39, pred[16,256]{1,0:T(8,128)(4,1)S(1)} %compare_and_fusion), kind=kOutput, calls=%fused_computation.37 | convolution fusion | flops 33882112 | bytes 1183744 | tf_op jit(solution)/shard_map/ejt,ekt->ekj/dot_general | solution.py:120
  91.0 4.3 %collective-permute-start.5 = (bf16[16,64,64]{1,2,0:T(8,128)(2,1)}, bf16[16,64,64]{1,2,0:T(8,128)(2,1)}, u32[]{:S(2)}, u32[]{:S(2)}) collective-permute-start(bf16[16,64,64]{1,2,0:T(8,128)(2,1)} %fusion.12), channel_id=1, source_target_pairs={{2,0},{4,2},{6,4},{8,6},{10,8},{12,10},{14,12},{0,14},{3,1},{5,3},... | collective-permute-start | bytes 393224 | tf_op jit(solution)/shard_map/ppermute | solution.py:22
  96.7 11.0 %psum.21 = bf16[64,64]{1,0:T(8,128)(2,1)S(1)} all-reduce(f32[64,64]{1,0:T(8,128)S(1)} %fusion.17), channel_id=1, replica_groups=mesh['groups'=2,'blk'=4,'leaf'=2,'sample'=2] {'leaf'}, use_global_device_ids=true, to_apply=%region_3.4 | all-reduce | flops 4096 | bytes 24576 | tf_op jit(solution)/shard_map/psum | solution.py:129
  107.7 13.5 %all-gather = bf16[256,64]{1,0:T(8,128)(2,1)S(1)} all-gather(bf16[64,64]{1,0:T(8,128)(2,1)S(1)} %psum.21), channel_id=2, replica_groups=mesh['groups'=2,'blk'=4,'leaf'=2,'sample'=2] {'blk'}, dimensions={0}, use_global_device_ids=true | all-gather | bytes 40960 | tf_op jit(solution)/shard_map/all_gather | solution.py:130
  124.5 3.1 %maximum_select_fusion = bf16[48,128,256]{2,0,1:T(8,128)(2,1)S(1)} fusion(bf16[48,64,256]{2,0,1:T(8,128)(2,1)} %collective-permute-done.2, bf16[48,64,256]{2,0,1:T(8,128)(2,1)} %slice.57, pred[]{:T(512)S(6)} %eq.12), kind=kLoop, calls=%fused_computation.28 | loop fusion | flops 4718592 | bytes 6291457 | tf_op jit(solution)/shard_map/jit(_where)/select_n | solution.py:81
  127.7 2.8 %copy.36 = bf16[48,128,256]{2,1,0:T(8,128)(2,1)} copy(bf16[48,128,256]{2,0,1:T(8,128)(2,1)S(1)} %maximum_select_fusion) | data formatting | bytes 6291456 | tf_op jit(solution)/shard_map/while | solution.py:108
  130.4 42.3 %while.12 = (s32[]{:T(128)}, f32[2,4,128,256]{3,2,1,0:T(8,128)}, s32[2]{0:T(128)S(1)}, s32[]{:T(128)}, s32[16,12]{1,0:T(8,128)}, /*index=5*/bf16[48,128,256]{2,1...) while((s32[]{:T(128)}, f32[2,4,128,256]{3,2,1,0:T(8,128)}, ...), condition=%wide.region_1.0_spmd, body=%wide.region_0.0_spmd.sunk | while | flops 852494208 | bytes 11184823 | solution.py:108
  134.2 4.4 %gather_fusion = bf16[48,128,256]{2,1,0:T(8,128)(2,1)} fusion(bf16[48,128,256]{2,1,0:T(8,128)(2,1)} %get-tuple-element.290, s32[1024]{0:T(1024)S(1)} %pad_clamp_fusion.4), kind=kCustom, calls=%fused_computation.clone.1 | custom fusion | bytes 6291648 | tf_op jit(solution)/shard_map/while/body/eval_jaxpr/gather | solution.py:95
  139.4 12.2 %fusion.54 = f32[2,4,128,256]{3,2,1,0:T(8,128)} fusion(f32[2,4,128,256]{3,2,1,0:T(8,128)} %get-tuple-element.270, s32[]{:T(128)} %get-tuple-element.269, bf16[4,12,128,256]{3,2,1,0:T(8,128)(2,1)} %bitcast.105, f32[4,12,256]{2,1,0:T(8,128)S(1)} %copy.62, f32[4,256]{1,0:T(4,128)S(1)} %get-tuple-element.248, f32[4,12,256]{2,1,0:T(8,128)S(1)} %copy.63, ...), kind=kOutput, calls=%fused_computation.8.clone.1 | convolution fusion | flops 852492288 | bytes 3830464 | tf_op jit(solution)/shard_map/while/body/eval_jaxpr/lkab,lksb->lsa/dot_general | solution.py:104
  155.4 4.4 %gather_fusion = bf16[48,128,256]{2,1,0:T(8,128)(2,1)} fusion(bf16[48,128,256]{2,1,0:T(8,128)(2,1)} %get-tuple-element.290, s32[1024]{0:T(1024)S(1)} %pad_clamp_fusion.4), kind=kCustom, calls=%fused_computation.clone.1 | custom fusion | bytes 6291648 | tf_op jit(solution)/shard_map/while/body/eval_jaxpr/gather | solution.py:95
  160.6 12.1 %fusion.54 = f32[2,4,128,256]{3,2,1,0:T(8,128)} fusion(f32[2,4,128,256]{3,2,1,0:T(8,128)} %get-tuple-element.270, s32[]{:T(128)} %get-tuple-element.269, bf16[4,12,128,256]{3,2,1,0:T(8,128)(2,1)} %bitcast.105, f32[4,12,256]{2,1,0:T(8,128)S(1)} %copy.62, f32[4,256]{1,0:T(4,128)S(1)} %get-tuple-element.248, f32[4,12,256]{2,1,0:T(8,128)S(1)} %copy.63, ...), kind=kOutput, calls=%fused_computation.8.clone.1 | convolution fusion | flops 852492288 | bytes 3830464 | tf_op jit(solution)/shard_map/while/body/eval_jaxpr/lkab,lksb->lsa/dot_general | solution.py:104
  172.7 1.8 dynamic-slice_convert_fusion
  176.8 2.1 gather_fusion.3
  179.0 1.9 constant_dynamic-slice_fusion
  181.9 4.6 %multiply_reduce_fusion.1 = (f32[64]{0:T(128)S(1)}, f32[16,64,256]{2,1,0:T(8,128)}) fusion(f32[16,64,256]{2,1,0:T(8,128)} %param.15, bf16[16,256,64]{1,2,0:T(8,128)(2,1)} %copy.39, pred[16,256]{1,0:T(8,128)(4,1)S(1)} %copy-done.12, f32[16,64,64]{2,1,0:T(8,128)} %convolution_bitcast_fusion.1, bf16[16,8,64,64]{2,3,1,0:T(8,128)(2,1)} %bitcast.107, ...), kind=kOutput, calls=%fused_computation.54 | convolution fusion | flops 103940032 | bytes 6558209 | tf_op jit(solution)/shard_map/bfw,baf->baw/dot_general | solution.py:148
  186.5 21.7 %all-reduce = (f32[64]{0:T(128)S(1)}, f32[64]{0:T(128)S(1)}) all-reduce(f32[64]{0:T(128)S(1)} %get-tuple-element.174, f32[64]{0:T(128)S(1)} %copy-done.14), channel_id=1, replica_groups=mesh['groups'=2,'blk'=4,'leaf'=2,'sample'=2] {'blk','leaf'}, use_global_device_ids=true, to_apply=%region_5.6 | all-reduce | flops 128 | bytes 1024 | tf_op jit(solution)/shard_map/psum | solution.py:154
  208.2 2.2 %fusion.23 = bf16[16,64,256]{2,1,0:T(8,128)(2,1)} fusion(f32[16,64,256]{2,1,0:T(8,128)} %get-tuple-element.175, bf16[16,64,256]{2,1,0:T(8,128)(2,1)S(1)} %copy-done.3, f32[64]{0:T(128)S(1)} %div.3), kind=kLoop, calls=%fused_computation.51 | loop fusion | flops 1048576 | bytes 2097408 | tf_op jit(solution)/shard_map/convert_element_type | solution.py:158
  (95 shorter events, 27.5 us)
Async XLA Ops:
  7.2 174.7 %copy-start = (bf16[16,8,64,64]{3,2,1,0:T(8,128)(2,1)S(1)}, bf16[16,8,64,64]{3,2,1,0:T(8,128)(2,1)}, u32[]{:S(2)}) copy-start(bf16[16,8,64,64]{3,2,1,0:T(8,128)(2,1)} %param.25) | copy-start | bytes 3145732
  7.2 37.5 %sort.19.cloned.1.call-start = ((), (), s32[]{:S(2)}) async-start(), calls=%async_computation | async-start | bytes 98336 | tf_op jit(solution)/shard_map/jit(argsort)/sort | solution.py:118
  10.1 31.2 %copy-start.1 = (bf16[16,67,256]{2,0,1:T(8,128)(2,1)}, bf16[16,67,256]{2,0,1:T(8,128)(2,1)S(1)}, u32[]{:S(2)}) copy-start(bf16[16,67,256]{2,0,1:T(8,128)(2,1)S(1)} %get-tuple-element.173) | copy-start | bytes 1646596
  10.1 26.4 %collective-permute-start = (bf16[16,67,256]{2,0,1:T(8,128)(2,1)S(1)}, bf16[16,67,256]{2,0,1:T(8,128)(2,1)S(1)}, u32[]{:S(2)}, u32[]{:S(2)}) collective-permute-start(bf16[16,67,256]{2,0,1:T(8,128)(2,1)S(1)} %get-tuple-element.173), channel_id=1, source_target_pairs={{0,2},{2,4},{4,6},{6,8},{8,10},{10,12},{12,14},{14,0},{1,3},{3,5},... | collective-permute-start | bytes 1646600 | tf_op jit(solution)/shard_map/ppermute | solution.py:21
  13.1 25.8 %collective-permute-start.1 = (bf16[16,67,256]{2,0,1:T(8,128)(2,1)S(1)}, bf16[16,67,256]{2,0,1:T(8,128)(2,1)}, u32[]{:S(2)}, u32[]{:S(2)}) collective-permute-start(bf16[16,67,256]{2,0,1:T(8,128)(2,1)S(1)} %get-tuple-element.173), channel_id=1, source_target_pairs={{2,0},{4,2},{6,4},{8,6},{10,8},{12,10},{14,12},{0,14},{3,1},{5,3},... | collective-permute-start | bytes 1646600 | tf_op jit(solution)/shard_map/ppermute | solution.py:22
  20.2 21.7 %copy-start.9 = (s32[16,12]{1,0:T(8,128)S(1)}, s32[16,12]{1,0:T(8,128)}, u32[]{:S(2)}) copy-start(s32[16,12]{1,0:T(8,128)} %param.23) | copy-start | bytes 2308
  36.5 4.8 %copy-start.4 = (bf16[16,67,256]{2,0,1:T(8,128)(2,1)}, bf16[16,67,256]{2,0,1:T(8,128)(2,1)S(1)}, u32[]{:S(2)}) copy-start(bf16[16,67,256]{2,0,1:T(8,128)(2,1)S(1)} %collective-permute-done) | copy-start | bytes 1646596
  41.3 83.2 %collective-permute-start.2 = (bf16[48,64,256]{2,0,1:T(8,128)(2,1)}, bf16[48,64,256]{2,0,1:T(8,128)(2,1)}, u32[]{:S(2)}, u32[]{:S(2)}) collective-permute-start(bf16[48,64,256]{2,0,1:T(8,128)(2,1)} %slice.57), channel_id=1, source_target_pairs={{0,1},{1,0},{2,3},{3,2},{4,5},{5,4},{6,7},{7,6},{8,9},{9,8},{10,11... | collective-permute-start | bytes 4718600 | tf_op jit(solution)/shard_map/ppermute | solution.py:28
  45.4 43.0 %copy-start.8 = (s32[16,256]{1,0:T(8,128)S(1)}, s32[16,256]{1,0:T(8,128)}, u32[]{:S(2)}) copy-start(s32[16,256]{1,0:T(8,128)} %get-tuple-element.131) | copy-start | bytes 49156
  45.4 50.0 %copy-start.7 = (bf16[1,64,64]{2,1,0:T(8,128)(2,1)S(1)}, bf16[1,64,64]{2,1,0:T(8,128)(2,1)}, u32[]{:S(2)}) copy-start(bf16[1,64,64]{2,1,0:T(8,128)(2,1)} %param.22) | copy-start | bytes 24580
  86.0 9.4 %copy-start.6 = (bf16[16,64,64]{2,1,0:T(8,128)(2,1)S(1)}, bf16[16,64,64]{2,1,0:T(8,128)(2,1)}, u32[]{:S(2)}) copy-start(bf16[16,64,64]{2,1,0:T(8,128)(2,1)} %param.21) | copy-start | bytes 393220
  86.0 37.7 %copy-start.2 = (bf16[16,67,256]{2,0,1:T(8,128)(2,1)S(1)}, bf16[16,67,256]{2,0,1:T(8,128)(2,1)}, u32[]{:S(2)}) copy-start(bf16[16,67,256]{2,0,1:T(8,128)(2,1)} %copy-done.1) | copy-start | bytes 1646596
  86.0 37.7 %copy-start.5 = (bf16[16,67,256]{2,0,1:T(8,128)(2,1)S(1)}, bf16[16,67,256]{2,0,1:T(8,128)(2,1)}, u32[]{:S(2)}) copy-start(bf16[16,67,256]{2,0,1:T(8,128)(2,1)} %copy-done.4) | copy-start | bytes 1646596
  88.4 2.6 %copy-start.11 = (pred[16,256]{1,0:T(8,128)(4,1)}, pred[16,256]{1,0:T(8,128)(4,1)S(1)}, u32[]{:S(2)}) copy-start(pred[16,256]{1,0:T(8,128)(4,1)S(1)} %compare_and_fusion) | copy-start | bytes 12292
  90.6 84.9 %collective-permute-start.4 = (bf16[16,64,64]{1,2,0:T(8,128)(2,1)}, bf16[16,64,64]{1,2,0:T(8,128)(2,1)}, u32[]{:S(2)}, u32[]{:S(2)}) collective-permute-start(bf16[16,64,64]{1,2,0:T(8,128)(2,1)} %fusion.12), channel_id=1, source_target_pairs={{0,2},{2,4},{4,6},{6,8},{8,10},{10,12},{12,14},{14,0},{1,3},{3,5},... | collective-permute-start | bytes 393224 | tf_op jit(solution)/shard_map/ppermute | solution.py:21
  91.0 84.5 %collective-permute-start.5 = (bf16[16,64,64]{1,2,0:T(8,128)(2,1)}, bf16[16,64,64]{1,2,0:T(8,128)(2,1)}, u32[]{:S(2)}, u32[]{:S(2)}) collective-permute-start(bf16[16,64,64]{1,2,0:T(8,128)(2,1)} %fusion.12), channel_id=1, source_target_pairs={{2,0},{4,2},{6,4},{8,6},{10,8},{12,10},{14,12},{0,14},{3,1},{5,3},... | collective-permute-start | bytes 393224 | tf_op jit(solution)/shard_map/ppermute | solution.py:22
  130.4 46.4 %copy-start.10 = (s32[1024]{0:T(1024)S(1)}, s32[1024]{0:T(1024)}, u32[]{:S(2)}) copy-start(s32[1024]{0:T(1024)} %pad_clamp_fusion.1) | copy-start | bytes 12292
  174.5 6.4 %collective-permute-start.3 = (bf16[8,64,256]{2,1,0:T(8,128)(2,1)}, bf16[8,64,256]{2,1,0:T(8,128)(2,1)}, u32[]{:S(2)}, u32[]{:S(2)}) collective-permute-start(bf16[8,64,256]{2,1,0:T(8,128)(2,1)} %dynamic-slice_convert_fusion), channel_id=1, source_target_pairs={{0,1},{1,0},{2,3},{3,2},{4,5},{5,4},{6,7},{7,6},{8,9},{9,8},{10,11... | collective-permute-start | bytes 786440 | tf_op jit(solution)/shard_map/ppermute | solution.py:28
  176.8 5.1 %copy-start.3 = (bf16[16,64,256]{2,1,0:T(8,128)(2,1)S(1)}, bf16[16,64,256]{2,1,0:T(8,128)(2,1)}, u32[]{:S(2)}) copy-start(bf16[16,64,256]{2,1,0:T(8,128)(2,1)} %param.16) | copy-start | bytes 1572868
  176.8 5.1 %copy-start.12 = (pred[16,256]{1,0:T(8,128)(4,1)S(1)}, pred[16,256]{1,0:T(8,128)(4,1)}, u32[]{:S(2)}) copy-start(pred[16,256]{1,0:T(8,128)(4,1)} %copy-done.11) | copy-start | bytes 12292
  176.8 5.1 %copy-start.13 = (f32[64]{0:T(128)S(1)}, f32[64]{0:T(128)}, u32[]{:S(2)}) copy-start(f32[64]{0:T(128)} %param.17) | copy-start | bytes 772
  181.9 4.6 %copy-start.14 = (f32[64]{0:T(128)S(1)}, f32[64]{0:T(128)}, u32[]{:S(2)}) copy-start(f32[64]{0:T(128)} %multiply_reduce_fusion) | copy-start | bytes 772
Sparse Core Ops, SparseCore 0:
  16.9 2.5 sort.21.cloned.1.call-done
  (1 shorter events, 0.0 us)
where the time goes:
time: 218 us; the launch traced here: 217 us
  local copies, waits for them, and re-layouts  71.6 us (33%)
  blocking collectives  46.2 us (21%)
  matrix products  34.6 us (16%)
  other arithmetic  19.7 us (9%)
  waiting for transfers between devices  18.7 us (9%)
  between operations  14.3 us (7%)
  starting transfers between devices  10.7 us (5%)
    gather x2, local copies, waits for them, and re-layouts, on_device(): natural_values = jnp.take_along_axis(basis, inverse[:, None, :], axis=2)  43 us
    dot_general x2, matrix products, near_block(): jnp.einsum('lkab,lksb->lsa', kernel_tiles, near_values, preferred_element...  24.3 us
    psum x1, blocking collectives, on_device(): new_norm = lax.psum(new_square, ('blk', 'leaf'))  21.7 us
    ppermute x2, waiting for transfers between devices, padded(): before = lax.ppermute(last, axis, up)  16.4 us
    all_gather x1, blocking collectives, on_device(): every_top = lax.all_gather(top_node[None], 'blk', axis=0, tiled=True)  13.5 us
    psum x1, blocking collectives, on_device(): top_node = lax.psum(lifted, 'leaf').astype(jnp.bfloat16)  11 us
    gather x2, local copies, waits for them, and re-layouts, near_block(): near_values = all_columns[slot_rows]  8.85 us
    ppermute x2, starting transfers between devices, padded(): after = lax.ppermute(initial, axis, down)  7.38 us
  transfers between devices with their start and end apart: 6, of which 2 were waited for; matrix products, arithmetic and copies ran while one was open for 52% of the time, Pallas kernels for 0%

commit v1 on v0

--- a/solution.py
+++ b/solution.py
@@ -9,6 +9,27 @@
 LENGTH = 0.3
 AMPLITUDE = 0.25
 NUGGET = 0.5
+
+
+def ring_gather(shard, axis, dim):
+    peers, index, rows = (lax.axis_size(axis), lax.axis_index(axis), shard.shape[dim])
+    right = [(i, (i + 1) % peers) for i in range(peers)]
+    behind = [(i, (i - 1) % peers) for i in range(peers)]
+    filled = jnp.zeros((*shard.shape[:dim], peers * rows, *shard.shape[dim + 1 :]), shard.dtype)
+    filled = lax.dynamic_update_slice_in_dim(filled, shard, index * rows, axis=dim)
+    from_left = from_right = shard
+    half = peers // 2
+    for turn in range(1, half + 1):
+        from_left = lax.ppermute(from_left, axis, right)
+        filled = lax.dynamic_update_slice_in_dim(
+            filled, from_left, (index - turn) % peers * rows, axis=dim
+        )
+        if turn < peers - half:
+            from_right = lax.ppermute(from_right, axis, behind)
+            filled = lax.dynamic_update_slice_in_dim(
+                filled, from_right, (index + turn) % peers * rows, axis=dim
+            )
+    return filled
 
 
 def padded(array, sides, width):
@@ -127,7 +148,7 @@
         "rk,sk->sr", node_transfer[0], node_coef, preferred_element_type=jnp.float32
     )
     top_node = lax.psum(lifted, "leaf").astype(jnp.bfloat16)
-    every_top = lax.all_gather(top_node[None], "blk", axis=0, tiled=True)
+    every_top = ring_gather(top_node[None], "blk", 0)
     chosen = every_top[top_list[0]]
     incoming = jnp.einsum(
         "krj,ksj->sr", top_coupling[0], chosen, preferred_element_type=jnp.float32

time: 218 us -> 201 us (0.922)
  blocking collectives: 46.2 us -> 24.3 us
  starting transfers between devices: 10.7 us -> 14.8 us
  waiting for transfers between devices: 18.7 us -> 20.9 us
    all_gather x1 -> x0, blocking collectives: 13.5 us -> none  [on_device(): every_top = lax.all_gather(top_node[None], 'blk', axis=0, tiled=True)]
    ppermute x0 -> x3, waiting for transfers between devices: none -> 5.48 us  [the longest x2 5.48 us: ring_gather(): from_left = lax.ppermute(from_left, axis, right)]
    psum x1, blocking collectives: 21.7 us -> 17.1 us  [on_device(): new_norm = lax.psum(new_square, ('blk', 'leaf'))]
    ppermute x0 -> x3, starting transfers between devices: none -> 4.11 us  [the longest x1 2.25 us: ring_gather(): from_right = lax.ppermute(from_right, axis, behind)]
    psum x1, blocking collectives: 11 us -> 7.15 us  [on_device(): top_node = lax.psum(lifted, 'leaf').astype(jnp.bfloat16)]
    ppermute x2, waiting for transfers between devices: 16.4 us -> 13.2 us  [padded(): before = lax.ppermute(last, axis, up)]
    unnamed x34 -> x28, local copies, waits for them, and re-layouts: 3.11 us -> 4.53 us
  transfers between devices with their start and end apart: 6 -> 9, of which waited for: 2 -> 3; matrix products, arithmetic and copies ran while one was open for 52% -> 55% of each run, Pallas kernels for 0% -> 0%
where the time goes in v1:
time: 201 us; the launch traced here: 200 us
  local copies, waits for them, and re-layouts  71.4 us (36%)
  matrix products  32.7 us (16%)
  blocking collectives  24.3 us (12%)
  waiting for transfers between devices  20.9 us (10%)
  other arithmetic  20 us (10%)
  starting transfers between devices  14.8 us (7%)
  between operations  14.4 us (7%)
    gather x2, local copies, waits for them, and re-layouts, on_device(): natural_values = jnp.take_along_axis(basis, inverse[:, None, :], axis=2)  42.1 us
    dot_general x2, matrix products, near_block(): jnp.einsum('lkab,lksb->lsa', kernel_tiles, near_values, preferred_element...  24.3 us
    psum x1, blocking collectives, on_device(): new_norm = lax.psum(new_square, ('blk', 'leaf'))  17.1 us
    ppermute x2, waiting for transfers between devices, padded(): before = lax.ppermute(last, axis, up)  13.2 us
    gather x2, local copies, waits for them, and re-layouts, near_block(): near_values = all_columns[slot_rows]  8.85 us
    psum x1, blocking collectives, on_device(): top_node = lax.psum(lifted, 'leaf').astype(jnp.bfloat16)  7.15 us
    ppermute x2, starting transfers between devices, padded(): after = lax.ppermute(initial, axis, down)  6.03 us
    ppermute x2, waiting for transfers between devices, ring_gather(): from_left = lax.ppermute(from_left, axis, right)  5.48 us
  transfers between devices with their start and end apart: 9, of which 3 were waited for; matrix products, arithmetic and copies ran while one was open for 55% of the time, Pallas kernels for 0%

profile of v1, /device:TPU:0, one launch (start us, length us, event | category | flops | bytes accessed | tf_op | source)
XLA Modules:
  0.0 200.0 jit_solution(10416384587022324397)
XLA Ops:
  7.2 2.3 %copy_dynamic-update-slice_fusion = bf16[16,67,256]{2,0,1:T(8,128)(2,1)} fusion(bf16[16,64,256]{2,1,0:T(8,128)(2,1)} %param.16), kind=kLoop, calls=%fused_computation.56 | loop fusion | bytes 1048576
  11.0 2.9 %collective-permute-start = (bf16[16,67,256]{2,0,1:T(8,128)(2,1)}, bf16[16,67,256]{2,0,1:T(8,128)(2,1)}, u32[]{:S(2)}, u32[]{:S(2)}) collective-permute-start(bf16[16,67,256]{2,0,1:T(8,128)(2,1)} %get-tuple-element.173), channel_id=1, source_target_pairs={{0,2},{2,4},{4,6},{6,8},{8,10},{10,12},{12,14},{14,0},{1,3},{3,5},... | collective-permute-start | bytes 1646600 | tf_op jit(solution)/shard_map/ppermute | solution.py:42
  13.9 3.0 %collective-permute-start.1 = (bf16[16,67,256]{2,0,1:T(8,128)(2,1)}, bf16[16,67,256]{2,0,1:T(8,128)(2,1)}, u32[]{:S(2)}, u32[]{:S(2)}) collective-permute-start(bf16[16,67,256]{2,0,1:T(8,128)(2,1)} %get-tuple-element.173), channel_id=1, source_target_pairs={{2,0},{4,2},{6,4},{8,6},{10,8},{12,10},{14,12},{0,14},{3,1},{5,3},... | collective-permute-start | bytes 1646600 | tf_op jit(solution)/shard_map/ppermute | solution.py:43
  21.9 2.0 multiply_reduce_fusion
  24.5 13.2 %collective-permute-done = bf16[16,67,256]{2,0,1:T(8,128)(2,1)} collective-permute-done((bf16[16,67,256]{2,0,1:T(8,128)(2,1)}, bf16[16,67,256]{2,0,1:T(8,128)(2,1)}, u32[]{:S(2)}, u32[]{:S(2)}) %collective-permute-start) | collective-permute-done | bytes 548896 | tf_op jit(solution)/shard_map/ppermute | solution.py:42
  37.7 2.2 %collective-permute-done.1 = bf16[16,67,256]{2,0,1:T(8,128)(2,1)} collective-permute-done((bf16[16,67,256]{2,0,1:T(8,128)(2,1)}, bf16[16,67,256]{2,0,1:T(8,128)(2,1)}, u32[]{:S(2)}, u32[]{:S(2)}) %collective-permute-start.1) | collective-permute-done | bytes 548896 | tf_op jit(solution)/shard_map/ppermute | solution.py:43
  43.4 40.6 %gather_fusion.4 = bf16[4096,64]{1,0:T(8,128)(2,1)} fusion(bf16[16,64,256]{1,2,0:T(8,128)(2,1)S(1)} %copy.38, s32[4096]{0:T(1024)S(1)} %bitcast.107), kind=kCustom, calls=%fused_computation.4 | custom fusion | bytes 1081344 | tf_op jit(solution)/shard_map/jit(take_along_axis)/gather | solution.py:140
  88.0 7.2 %psum.21 = bf16[64,64]{1,0:T(8,128)(2,1)S(1)} all-reduce(f32[64,64]{1,0:T(8,128)S(1)} %fusion.17), channel_id=1, replica_groups=mesh['groups'=2,'blk'=4,'leaf'=2,'sample'=2] {'leaf'}, use_global_device_ids=true, to_apply=%region_3.4 | all-reduce | flops 4096 | bytes 24576 | tf_op jit(solution)/shard_map/psum | solution.py:150
  96.7 2.3 %collective-permute-start.5 = (bf16[1,64,64]{2,1,0:T(8,128)(2,1)S(1)}, bf16[1,64,64]{2,1,0:T(8,128)(2,1)S(1)}, u32[]{:S(2)}, u32[]{:S(2)}) collective-permute-start(bf16[1,64,64]{2,1,0:T(8,128)(2,1)S(1)} %bitcast.116), channel_id=1, source_target_pairs={{0,12},{4,0},{8,4},{12,8},{1,13},{5,1},{9,5},{13,9},{2,14},{6,2},{... | collective-permute-start | bytes 24584 | tf_op jit(solution)/shard_map/ppermute | solution.py:28
  100.7 3.0 %collective-permute-start.8 = (bf16[16,64,64]{1,2,0:T(8,128)(2,1)S(1)}, bf16[16,64,64]{1,2,0:T(8,128)(2,1)}, u32[]{:S(2)}, u32[]{:S(2)}) collective-permute-start(bf16[16,64,64]{1,2,0:T(8,128)(2,1)S(1)} %fusion.12), channel_id=1, source_target_pairs={{2,0},{4,2},{6,4},{8,6},{10,8},{12,10},{14,12},{0,14},{3,1},{5,3},... | collective-permute-start | bytes 393224 | tf_op jit(solution)/shard_map/ppermute | solution.py:43
  104.1 5.5 %collective-permute-done.6 = bf16[1,64,64]{2,1,0:T(8,128)(2,1)S(1)} collective-permute-done((bf16[1,64,64]{2,1,0:T(8,128)(2,1)S(1)}, bf16[1,64,64]{2,1,0:T(8,128)(2,1)S(1)}, u32[]{:S(2)}, u32[]{:S(2)}) %collective-permute-start.6) | collective-permute-done | bytes 8224 | tf_op jit(solution)/shard_map/ppermute | solution.py:23
  112.2 3.1 %maximum_select_fusion = bf16[48,128,256]{2,0,1:T(8,128)(2,1)S(1)} fusion(bf16[48,64,256]{2,0,1:T(8,128)(2,1)} %collective-permute-done.2, bf16[48,64,256]{2,0,1:T(8,128)(2,1)} %slice.57, pred[]{:T(512)S(6)} %eq.16), kind=kLoop, calls=%fused_computation.28 | loop fusion | flops 4718592 | bytes 6291457 | tf_op jit(solution)/shard_map/jit(_where)/select_n | solution.py:102
  115.3 2.8 %copy.36 = bf16[48,128,256]{2,1,0:T(8,128)(2,1)} copy(bf16[48,128,256]{2,0,1:T(8,128)(2,1)S(1)} %maximum_select_fusion) | data formatting | bytes 6291456 | tf_op jit(solution)/shard_map/while | solution.py:129
  118.1 42.0 %while.12 = (s32[]{:T(128)}, f32[2,4,128,256]{3,2,1,0:T(8,128)}, s32[2]{0:T(128)S(1)}, s32[]{:T(128)}, s32[16,12]{1,0:T(8,128)}, /*index=5*/bf16[48,128,256]{2,1...) while((s32[]{:T(128)}, f32[2,4,128,256]{3,2,1,0:T(8,128)}, ...), condition=%wide.region_1.0_spmd, body=%wide.region_0.0_spmd.sunk | while | flops 852494208 | bytes 11184823 | solution.py:129
  121.8 4.4 %gather_fusion = bf16[48,128,256]{2,1,0:T(8,128)(2,1)} fusion(bf16[48,128,256]{2,1,0:T(8,128)(2,1)} %get-tuple-element.290, s32[1024]{0:T(1024)S(1)} %pad_clamp_fusion.4), kind=kCustom, calls=%fused_computation.clone.1 | custom fusion | bytes 6291648 | tf_op jit(solution)/shard_map/while/body/eval_jaxpr/gather | solution.py:116
  127.0 12.2 %fusion.54 = f32[2,4,128,256]{3,2,1,0:T(8,128)} fusion(f32[2,4,128,256]{3,2,1,0:T(8,128)} %get-tuple-element.270, s32[]{:T(128)} %get-tuple-element.269, bf16[4,12,128,256]{3,2,1,0:T(8,128)(2,1)} %bitcast.108, f32[4,12,256]{2,1,0:T(8,128)S(1)} %copy.62, f32[4,256]{1,0:T(4,128)S(1)} %get-tuple-element.248, f32[4,12,256]{2,1,0:T(8,128)S(1)} %copy.63, ...), kind=kOutput, calls=%fused_computation.8.clone.1 | convolution fusion | flops 852492288 | bytes 3830464 | tf_op jit(solution)/shard_map/while/body/eval_jaxpr/lkab,lksb->lsa/dot_general | solution.py:125
  142.8 4.4 %gather_fusion = bf16[48,128,256]{2,1,0:T(8,128)(2,1)} fusion(bf16[48,128,256]{2,1,0:T(8,128)(2,1)} %get-tuple-element.290, s32[1024]{0:T(1024)S(1)} %pad_clamp_fusion.4), kind=kCustom, calls=%fused_computation.clone.1 | custom fusion | bytes 6291648 | tf_op jit(solution)/shard_map/while/body/eval_jaxpr/gather | solution.py:116
  148.0 12.1 %fusion.54 = f32[2,4,128,256]{3,2,1,0:T(8,128)} fusion(f32[2,4,128,256]{3,2,1,0:T(8,128)} %get-tuple-element.270, s32[]{:T(128)} %get-tuple-element.269, bf16[4,12,128,256]{3,2,1,0:T(8,128)(2,1)} %bitcast.108, f32[4,12,256]{2,1,0:T(8,128)S(1)} %copy.62, f32[4,256]{1,0:T(4,128)S(1)} %get-tuple-element.248, f32[4,12,256]{2,1,0:T(8,128)S(1)} %copy.63, ...), kind=kOutput, calls=%fused_computation.8.clone.1 | convolution fusion | flops 852492288 | bytes 3830464 | tf_op jit(solution)/shard_map/while/body/eval_jaxpr/lkab,lksb->lsa/dot_general | solution.py:125
  160.1 1.8 dynamic-slice_convert_fusion
  164.1 2.1 %gather_fusion.3 = bf16[128,64,64]{1,2,0:T(8,128)(2,1)} fusion(bf16[48,64,64]{1,2,0:T(8,128)(2,1)S(1)} %pad_maximum_fusion.1, s32[1024]{0:T(1024)S(1)} %copy-done.7), kind=kCustom, calls=%fused_computation.3 | custom fusion | bytes 2097664 | tf_op jit(solution)/shard_map/gather | solution.py:161
  166.3 1.9 constant_dynamic-slice_fusion
  169.2 4.6 %multiply_reduce_fusion.1 = (f32[64]{0:T(128)S(1)}, f32[16,64,256]{2,1,0:T(8,128)}) fusion(f32[16,64,256]{2,1,0:T(8,128)} %param.15, bf16[16,256,64]{1,2,0:T(8,128)(2,1)} %copy-done.2, pred[16,256]{1,0:T(8,128)(4,1)S(1)} %copy-done.9, f32[16,64,64]{2,1,0:T(8,128)} %convolution_bitcast_fusion.1, bf16[16,8,64,64]{2,3,1,0:T(8,128)(2,1)} %bitcast.110, ...), kind=kOutput, calls=%fused_computation.54 | convolution fusion | flops 103940032 | bytes 6558209 | tf_op jit(solution)/shard_map/bfw,baf->baw/dot_general | solution.py:169
  173.8 17.1 %all-reduce = (f32[64]{0:T(128)S(1)}, f32[64]{0:T(128)S(1)}) all-reduce(f32[64]{0:T(128)S(1)} %get-tuple-element.174, f32[64]{0:T(128)S(1)} %copy-done.11), channel_id=1, replica_groups=mesh['groups'=2,'blk'=4,'leaf'=2,'sample'=2] {'blk','leaf'}, use_global_device_ids=true, to_apply=%region_5.6 | all-reduce | flops 128 | bytes 1024 | tf_op jit(solution)/shard_map/psum | solution.py:175
  190.9 2.2 %fusion.23 = bf16[16,64,256]{2,1,0:T(8,128)(2,1)} fusion(f32[16,64,256]{2,1,0:T(8,128)} %get-tuple-element.175, bf16[16,64,256]{2,1,0:T(8,128)(2,1)S(1)} %copy-done.1, f32[64]{0:T(128)S(1)} %div.3), kind=kLoop, calls=%fused_computation.51 | loop fusion | flops 1048576 | bytes 2097408 | tf_op jit(solution)/shard_map/convert_element_type | solution.py:179
  (99 shorter events, 31.3 us)
Async XLA Ops:
  7.2 162.0 %copy-start = (bf16[16,8,64,64]{3,2,1,0:T(8,128)(2,1)S(1)}, bf16[16,8,64,64]{3,2,1,0:T(8,128)(2,1)}, u32[]{:S(2)}) copy-start(bf16[16,8,64,64]{3,2,1,0:T(8,128)(2,1)} %param.25) | copy-start | bytes 3145732
  7.2 16.7 %copy-start.6 = (s32[16,12]{1,0:T(8,128)S(1)}, s32[16,12]{1,0:T(8,128)}, u32[]{:S(2)}) copy-start(s32[16,12]{1,0:T(8,128)} %param.23) | copy-start | bytes 2308
  7.2 35.5 %sort.19.cloned.1.call-start = ((), (), s32[]{:S(2)}) async-start(), calls=%async_computation | async-start | bytes 98336 | tf_op jit(solution)/shard_map/jit(argsort)/sort | solution.py:139
  11.0 26.7 %collective-permute-start = (bf16[16,67,256]{2,0,1:T(8,128)(2,1)}, bf16[16,67,256]{2,0,1:T(8,128)(2,1)}, u32[]{:S(2)}, u32[]{:S(2)}) collective-permute-start(bf16[16,67,256]{2,0,1:T(8,128)(2,1)} %get-tuple-element.173), channel_id=1, source_target_pairs={{0,2},{2,4},{4,6},{6,8},{8,10},{10,12},{12,14},{14,0},{1,3},{3,5},... | collective-permute-start | bytes 1646600 | tf_op jit(solution)/shard_map/ppermute | solution.py:42
  13.9 26.0 %collective-permute-start.1 = (bf16[16,67,256]{2,0,1:T(8,128)(2,1)}, bf16[16,67,256]{2,0,1:T(8,128)(2,1)}, u32[]{:S(2)}, u32[]{:S(2)}) collective-permute-start(bf16[16,67,256]{2,0,1:T(8,128)(2,1)} %get-tuple-element.173), channel_id=1, source_target_pairs={{2,0},{4,2},{6,4},{8,6},{10,8},{12,10},{14,12},{0,14},{3,1},{5,3},... | collective-permute-start | bytes 1646600 | tf_op jit(solution)/shard_map/ppermute | solution.py:43
  42.7 69.6 %collective-permute-start.2 = (bf16[48,64,256]{2,0,1:T(8,128)(2,1)}, bf16[48,64,256]{2,0,1:T(8,128)(2,1)}, u32[]{:S(2)}, u32[]{:S(2)}) collective-permute-start(bf16[48,64,256]{2,0,1:T(8,128)(2,1)} %slice.57), channel_id=1, source_target_pairs={{0,1},{1,0},{2,3},{3,2},{4,5},{5,4},{6,7},{7,6},{8,9},{9,8},{10,11... | collective-permute-start | bytes 4718600 | tf_op jit(solution)/shard_map/ppermute | solution.py:49
  43.4 42.2 %copy-start.5 = (s32[16,256]{1,0:T(8,128)S(1)}, s32[16,256]{1,0:T(8,128)}, u32[]{:S(2)}) copy-start(s32[16,256]{1,0:T(8,128)} %get-tuple-element.131) | copy-start | bytes 49156
  43.4 44.2 %copy-start.4 = (bf16[1,64,64]{2,1,0:T(8,128)(2,1)S(1)}, bf16[1,64,64]{2,1,0:T(8,128)(2,1)}, u32[]{:S(2)}) copy-start(bf16[1,64,64]{2,1,0:T(8,128)(2,1)} %param.22) | copy-start | bytes 24580
  84.0 3.6 %copy-start.3 = (bf16[16,64,64]{2,1,0:T(8,128)(2,1)S(1)}, bf16[16,64,64]{2,1,0:T(8,128)(2,1)}, u32[]{:S(2)}) copy-start(bf16[16,64,64]{2,1,0:T(8,128)(2,1)} %param.21) | copy-start | bytes 393220
  85.6 25.8 %copy-start.2 = (bf16[16,256,64]{1,2,0:T(8,128)(2,1)}, bf16[16,256,64]{1,2,0:T(8,128)(2,1)S(1)}, u32[]{:S(2)}) copy-start(bf16[16,256,64]{1,2,0:T(8,128)(2,1)S(1)} %copy.39) | copy-start | bytes 1572868
  85.6 0.6 copy-start.8
  95.1 8.6 %collective-permute-start.4 = (bf16[1,64,64]{2,1,0:T(8,128)(2,1)S(1)}, bf16[1,64,64]{2,1,0:T(8,128)(2,1)S(1)}, u32[]{:S(2)}, u32[]{:S(2)}) collective-permute-start(bf16[1,64,64]{2,1,0:T(8,128)(2,1)S(1)} %bitcast.115), channel_id=1, source_target_pairs={{0,4},{4,8},{8,12},{12,0},{1,5},{5,9},{9,13},{13,1},{2,6},{6,10},{... | collective-permute-start | bytes 24584 | tf_op jit(solution)/shard_map/ppermute | solution.py:23
  96.7 7.3 %collective-permute-start.5 = (bf16[1,64,64]{2,1,0:T(8,128)(2,1)S(1)}, bf16[1,64,64]{2,1,0:T(8,128)(2,1)S(1)}, u32[]{:S(2)}, u32[]{:S(2)}) collective-permute-start(bf16[1,64,64]{2,1,0:T(8,128)(2,1)S(1)} %bitcast.116), channel_id=1, source_target_pairs={{0,12},{4,0},{8,4},{12,8},{1,13},{5,1},{9,5},{13,9},{2,14},{6,2},{... | collective-permute-start | bytes 24584 | tf_op jit(solution)/shard_map/ppermute | solution.py:28
  99.0 63.9 %collective-permute-start.7 = (bf16[16,64,64]{1,2,0:T(8,128)(2,1)S(1)}, bf16[16,64,64]{1,2,0:T(8,128)(2,1)S(1)}, u32[]{:S(2)}, u32[]{:S(2)}) collective-permute-start(bf16[16,64,64]{1,2,0:T(8,128)(2,1)S(1)} %fusion.12), channel_id=1, source_target_pairs={{0,2},{2,4},{4,6},{6,8},{8,10},{10,12},{12,14},{14,0},{1,3},{3,5},... | collective-permute-start | bytes 393224 | tf_op jit(solution)/shard_map/ppermute | solution.py:42
  100.7 62.2 %collective-permute-start.8 = (bf16[16,64,64]{1,2,0:T(8,128)(2,1)S(1)}, bf16[16,64,64]{1,2,0:T(8,128)(2,1)}, u32[]{:S(2)}, u32[]{:S(2)}) collective-permute-start(bf16[16,64,64]{1,2,0:T(8,128)(2,1)S(1)} %fusion.12), channel_id=1, source_target_pairs={{2,0},{4,2},{6,4},{8,6},{10,8},{12,10},{14,12},{0,14},{3,1},{5,3},... | collective-permute-start | bytes 393224 | tf_op jit(solution)/shard_map/ppermute | solution.py:43
  103.8 5.8 %collective-permute-start.6 = (bf16[1,64,64]{2,1,0:T(8,128)(2,1)S(1)}, bf16[1,64,64]{2,1,0:T(8,128)(2,1)S(1)}, u32[]{:S(2)}, u32[]{:S(2)}) collective-permute-start(bf16[1,64,64]{2,1,0:T(8,128)(2,1)S(1)} %collective-permute-done.4), channel_id=1, source_target_pairs={{0,4},{4,8},{8,12},{12,0},{1,5},{5,9},{9,13},{13,1},{2,6},{6,10},{... | collective-permute-start | bytes 24584 | tf_op jit(solution)/shard_map/ppermute | solution.py:23
  118.1 46.0 %copy-start.7 = (s32[1024]{0:T(1024)S(1)}, s32[1024]{0:T(1024)}, u32[]{:S(2)}) copy-start(s32[1024]{0:T(1024)} %pad_clamp_fusion.1) | copy-start | bytes 12292
  161.9 6.2 %collective-permute-start.3 = (bf16[8,64,256]{2,1,0:T(8,128)(2,1)}, bf16[8,64,256]{2,1,0:T(8,128)(2,1)}, u32[]{:S(2)}, u32[]{:S(2)}) collective-permute-start(bf16[8,64,256]{2,1,0:T(8,128)(2,1)} %dynamic-slice_convert_fusion), channel_id=1, source_target_pairs={{0,1},{1,0},{2,3},{3,2},{4,5},{5,4},{6,7},{7,6},{8,9},{9,8},{10,11... | collective-permute-start | bytes 786440 | tf_op jit(solution)/shard_map/ppermute | solution.py:49
  164.1 5.1 %copy-start.1 = (bf16[16,64,256]{2,1,0:T(8,128)(2,1)S(1)}, bf16[16,64,256]{2,1,0:T(8,128)(2,1)}, u32[]{:S(2)}) copy-start(bf16[16,64,256]{2,1,0:T(8,128)(2,1)} %param.16) | copy-start | bytes 1572868
  164.1 5.1 %copy-start.9 = (pred[16,256]{1,0:T(8,128)(4,1)S(1)}, pred[16,256]{1,0:T(8,128)(4,1)}, u32[]{:S(2)}) copy-start(pred[16,256]{1,0:T(8,128)(4,1)} %copy-done.8) | copy-start | bytes 12292
  164.1 5.1 %copy-start.10 = (f32[64]{0:T(128)S(1)}, f32[64]{0:T(128)}, u32[]{:S(2)}) copy-start(f32[64]{0:T(128)} %param.17) | copy-start | bytes 772
  169.2 4.6 %copy-start.11 = (f32[64]{0:T(128)S(1)}, f32[64]{0:T(128)}, u32[]{:S(2)}) copy-start(f32[64]{0:T(128)} %multiply_reduce_fusion) | copy-start | bytes 772
Sparse Core Ops, SparseCore 0:
  17.7 2.5 sort.21.cloned.1.call-done
  (1 shorter events, 0.0 us)
